TPU v7x, 32 devices: a whole 2x2x4 slice. The times are simulated.
32 devices in a mesh: grp: 2 (over y), seq: 4 (over z), head: 4 (over x, core).
Axes of the slice: x: 2, y: 2, z: 4, core: 2. Of those that a mesh axis runs over, the one named last changes fastest.
Arguments:
- encoder: bfloat16 [8, 256, 4096], P('grp', 'seq'), parts along dimension 0, may hold values from -6 to 6
- key_weight: bfloat16 [4096, 4096], P('seq', 'head'), may hold values from -0.09375 to 0.09375
- value_weight: bfloat16 [4096, 4096], P('seq', 'head'), may hold values from -0.09375 to 0.09375
- tile_mask: int32 [2, 64, 64], P(None, 'seq', 'head'), may hold values 0 or 1
- lengths: int32 [8], P('grp'), parts along dimension 0, may hold values from 64 to 256, as said below
- queries: bfloat16 [8, 64, 4096], P('grp', 'seq', 'head'), parts along dimension 0, may hold values from -240 to 240
- cotangent: bfloat16 [8, 64, 4096], P('grp', 'seq', 'head'), parts along dimension 0, may hold values from -6 to 6
Outputs:
- attention: bfloat16 [8, 64, 4096], P('grp', 'seq', 'head'), parts along dimension 0
- query_grad: bfloat16 [8, 64, 4096], P('grp', 'seq', 'head'), parts along dimension 0
- encoder_grad: bfloat16 [8, 256, 4096], P('grp', 'seq', 'head'), parts along dimension 0
There are 2 independent parts, one for each index of `grp`. A program takes and returns all parts, laid end to end along the dimension named above; an argument that names none is the same for every part. Nothing has to cross between parts.
Inputs may be any that keep to these rules, and one draw needn't show every extreme that they name: `lengths`: one document of each group has all 256 positions valid.
All inputs are finite; a program needn't handle non-finite values. No bound on the sum of `tile_mask` on one device may be relied on, other than what follows from the above.
Results may differ from a plain program's by a relative error of at most 0.0096.
Values may be sent and summed in bfloat16 or wider, within the bound.
No kernel may reach another device: no remote copies, remote signals or barrier semaphores. Data moves between devices by JAX's collectives and lax.ppermute only.
A program may use at most 128 MiB of HBM per device.

v0:
```python
import jax
import jax.numpy as jnp
from jax import lax
from jax.sharding import PartitionSpec as P

DH = 64
TILE = 64
DOCS = 4
SCALE = 0.125
FLOOR_SCORE = -1e30


def expand(tile_grid, tile_edge):
    return jnp.repeat(jnp.repeat(tile_grid, tile_edge, axis=0), tile_edge, axis=1)


def attend(keys, values, queries, cotangent, length):
    position = jnp.arange(keys.shape[0])[None, :]
    live = position < length
    scores = jnp.dot(queries, keys.T, preferred_element_type=jnp.float32) * SCALE
    scores = jnp.where(live, scores, FLOOR_SCORE)
    row_max = jnp.max(scores, axis=1, keepdims=True)
    weights = jnp.where(live, jnp.exp(scores - row_max), 0.0)
    probs = weights / jnp.sum(weights, axis=1, keepdims=True)
    probs_low = probs.astype(jnp.bfloat16)
    output = jnp.dot(probs_low, values, preferred_element_type=jnp.float32)
    delta = jnp.sum(cotangent.astype(jnp.float32) * output, axis=1, keepdims=True)
    prob_grad = jnp.dot(cotangent, values.T, preferred_element_type=jnp.float32)
    score_grad = (probs * (prob_grad - delta) * SCALE).astype(jnp.bfloat16)
    query_grad = jnp.dot(score_grad, keys, preferred_element_type=jnp.float32)
    key_grad = jnp.dot(score_grad.T, queries, preferred_element_type=jnp.float32)
    value_grad = jnp.dot(probs_low.T, cotangent, preferred_element_type=jnp.float32)
    return (
        output.astype(jnp.bfloat16),
        query_grad.astype(jnp.bfloat16),
        key_grad.astype(jnp.bfloat16),
        value_grad.astype(jnp.bfloat16),
    )


def project(encoder, key_piece, value_piece):
    count = key_piece.shape[0]
    flat = encoder.reshape(DOCS * encoder.shape[1], count)
    key_flat = jnp.dot(flat, key_piece, preferred_element_type=jnp.float32)
    value_flat = jnp.dot(flat, value_piece, preferred_element_type=jnp.float32)
    shape_out = (DOCS, encoder.shape[1], key_piece.shape[1])
    return (key_flat.reshape(shape_out), value_flat.reshape(shape_out))


def back_product(key_rows, value_rows, key_piece, value_piece):
    contract = (((1,), (1,)), ((), ()))
    total = lax.dot_general(key_rows, key_piece, contract, preferred_element_type=jnp.float32)
    return total + lax.dot_general(
        value_rows, value_piece, contract, preferred_element_type=jnp.float32
    )


def body(encoder, key_weight, value_weight, tile_mask, lengths, queries, cotangent):
    seq_count = lax.axis_size("seq")
    enc_rows = encoder.shape[1]
    dec_rows = queries.shape[1]
    group_heads = queries.shape[2] // DH
    pair_count = DOCS * group_heads
    local_pairs = pair_count // seq_count
    key_masked = key_weight * expand(tile_mask[0], TILE).astype(jnp.bfloat16)
    value_masked = value_weight * expand(tile_mask[1], TILE).astype(jnp.bfloat16)
    full_key, full_value = (
        lax.all_gather(key_masked, "seq", axis=0, tiled=True),
        lax.all_gather(value_masked, "seq", axis=0, tiled=True),
    )
    key_sum, value_sum = project(encoder, full_key, full_value)

    def to_pairs(first, second, rows):
        joined = jnp.concatenate(
            [
                first.reshape(DOCS, rows, group_heads, DH),
                second.reshape(DOCS, rows, group_heads, DH),
            ],
            axis=3,
        )
        return joined.transpose(0, 2, 1, 3).reshape(pair_count, rows, 2 * DH)

    def from_pairs(block, rows):
        shaped = block.reshape(DOCS, group_heads, rows, 2 * DH).transpose(0, 2, 1, 3)
        first = shaped[..., :DH].reshape(DOCS, rows, group_heads * DH)
        second = shaped[..., DH:].reshape(DOCS, rows, group_heads * DH)
        return (first, second)

    query_pairs = to_pairs(queries, cotangent, dec_rows)
    query_owned = lax.all_to_all(query_pairs, "seq", split_axis=0, concat_axis=1, tiled=True)
    kv_pairs = to_pairs(key_sum.astype(jnp.bfloat16), value_sum.astype(jnp.bfloat16), enc_rows)
    kv_owned = lax.all_to_all(kv_pairs, "seq", split_axis=0, concat_axis=1, tiled=True)
    pair_ids = lax.axis_index("seq") * local_pairs + jnp.arange(local_pairs)
    doc_of_pair = pair_ids // group_heads
    pair_length = jnp.sum(
        jnp.where(doc_of_pair[:, None] == jnp.arange(DOCS)[None, :], lengths[None, :], 0), axis=1
    )

    def owner_pair(items):
        pair_kv, pair_query, length = items
        output, query_grad, key_grad, value_grad = attend(
            pair_kv[:, :DH], pair_kv[:, DH:], pair_query[:, :DH], pair_query[:, DH:], length
        )
        return (
            jnp.concatenate([output, query_grad], axis=1),
            jnp.concatenate([key_grad, value_grad], axis=1),
        )

    front, back = lax.map(owner_pair, (kv_owned, query_owned, pair_length))
    front_rows, back_rows = (
        lax.all_to_all(front, "seq", split_axis=1, concat_axis=0, tiled=True),
        lax.all_to_all(back, "seq", split_axis=1, concat_axis=0, tiled=True),
    )
    attention, query_grad = from_pairs(front_rows, dec_rows)
    key_grads, value_grads = from_pairs(back_rows, enc_rows)
    key_rows = key_grads.reshape(DOCS * enc_rows, group_heads * DH)
    value_rows = value_grads.reshape(DOCS * enc_rows, group_heads * DH)
    grad_terms = back_product(key_rows, value_rows, full_key, full_value)
    grad_share = lax.psum_scatter(grad_terms, "head", scatter_dimension=1, tiled=True)
    encoder_grad = grad_share.astype(jnp.bfloat16).reshape(DOCS, enc_rows, grad_share.shape[1])
    return (attention, query_grad, encoder_grad)


def solution(mesh):
    placed = (
        P("grp", "seq", None),
        P("seq", "head"),
        P("seq", "head"),
        P(None, "seq", "head"),
        P("grp"),
        P("grp", "seq", "head"),
        P("grp", "seq", "head"),
    )
    return jax.shard_map(
        body,
        mesh=mesh,
        in_specs=placed,
        out_specs=(P("grp", "seq", "head"), P("grp", "seq", "head"), P("grp", "seq", "head")),
        check_vma=False,
    )
```

profile of v0, /device:TPU:0, one launch (start us, length us, event | category | flops | bytes accessed | tf_op | source)
XLA Modules:
  0.0 557.6 jit_solution(13570915106982386981)
XLA Ops:
  7.2 0.9 convert.4
  8.4 3.9 copy.49
  12.3 3.1 bitcast_multiply_fusion.1
  15.8 3.9 copy.51
  19.7 3.1 bitcast_multiply_fusion
  22.8 0.9 copy-done.3
  24.2 0.8 copy.46
  25.0 6.3 %all-to-all-start = ((bf16[64,16,128]{2,1,0:T(8,128)(2,1)}), bf16[64,16,128]{2,1,0:T(8,128)(2,1)S(1)}, u32[]{:S(2)}, u32[]{:S(2)}) async-start(bf16[64,16,128]{2,1,0:T(8,128)(2,1)} %bitcast.6), calls=%async_computation | async-start | bytes 524288 | tf_op jit(solution)/shard_map/all_to_all | solution.py:90
  31.3 142.1 %all-gather.3.cloned.1.call-done = bf16[4096,1024]{0,1:T(8,128)(2,1)} async-done(((bf16[1024,1024]{0,1:T(8,128)(2,1)}), bf16[4096,1024]{0,1:T(8,128)(2,1)}) %all-gather.3.cloned.1.call-update) | async-done | bytes 8388624 | tf_op jit(solution)/shard_map/all_gather | solution.py:68
  173.5 5.7 %fusion.21 = bf16[256,1024]{0,1:T(8,128)(2,1)S(1)} fusion(bf16[4096,1024]{0,1:T(8,128)(2,1)} %all-gather.3.cloned.1.call-done, bf16[256,4096]{1,0:T(8,128)(2,1)S(1)} %bitcast.87), kind=kOutput, calls=%fused_computation.36 | convolution fusion | flops 2147745792 | bytes 11010048 | tf_op jit(solution)/shard_map/dot_general | solution.py:44
  179.2 143.6 %all-gather.5.cloned.1.call-done = bf16[4096,1024]{0,1:T(8,128)(2,1)} async-done(((bf16[1024,1024]{0,1:T(8,128)(2,1)}), bf16[4096,1024]{0,1:T(8,128)(2,1)}) %all-gather.5.cloned.1.call-update) | async-done | bytes 8388624 | tf_op jit(solution)/shard_map/all_gather | solution.py:69
  322.9 6.5 %fusion.22 = bf16[256,1024]{0,1:T(8,128)(2,1)} fusion(bf16[4096,1024]{0,1:T(8,128)(2,1)} %all-gather.5.cloned.1.call-done, bf16[256,4096]{1,0:T(8,128)(2,1)S(1)} %bitcast.88), kind=kOutput, calls=%fused_computation.37 | convolution fusion | flops 2147745792 | bytes 11010048 | tf_op jit(solution)/shard_map/dot_general | solution.py:45
  329.4 1.4 convert_element_type.73
  330.8 1.7 copy.52
  332.6 2.8 convert_element_type.79
  335.3 2.4 copy.53
  337.7 2.8 pad_maximum_fusion
  340.6 3.5 all-to-all-start.1
  345.0 25.3 %all-to-all-done.1 = bf16[64,64,128]{2,1,0:T(8,128)(2,1)S(1)} async-done(((bf16[64,64,128]{2,1,0:T(8,128)(2,1)}), bf16[64,64,128]{2,1,0:T(8,128)(2,1)S(1)}, u32[]{:S(2)}, u32[]{:S(2)}) %all-to-all-start.1) | async-done | bytes 1048608 | tf_op jit(solution)/shard_map/all_to_all | solution.py:92
  370.3 1.1 copy.54
  371.3 83.0 %while.12 = (s32[]{:T(128)}, bf16[16,64,128]{2,1,0:T(8,128)(2,1)S(1)}, bf16[16,256,128]{1,2,0:T(8,128)(2,1)}, s32[16]{0:T(128)S(1)}, bf16[16,64,128]{2,1,0:T(8,1...) while((s32[]{:T(128)}, bf16[16,64,128]{2,1,0:T(8,128)(2,1)S(1)}, bf16[16,256,128]{1,2,0:T(8,128)(2,1)}, ...), condition=%wide.region_5.6_spmd, body=%wide.region_1.5_spmd.sunk | while | flops 13144130 | bytes 1192309 | solution.py:109
  372.6 0.7 dynamic-slice_bitcast_fusion.5
  373.3 0.8 dynamic-slice_bitcast_fusion.4
  377.8 0.7 dynamic-slice_bitcast_fusion.5
  378.5 0.8 dynamic-slice_bitcast_fusion.4
  383.0 0.7 dynamic-slice_bitcast_fusion.5
  383.7 0.8 dynamic-slice_bitcast_fusion.4
  388.2 0.7 dynamic-slice_bitcast_fusion.5
  388.9 0.8 dynamic-slice_bitcast_fusion.4
  393.3 0.7 dynamic-slice_bitcast_fusion.5
  394.1 0.8 dynamic-slice_bitcast_fusion.4
  398.5 0.7 dynamic-slice_bitcast_fusion.5
  399.3 0.8 dynamic-slice_bitcast_fusion.4
  403.7 0.7 dynamic-slice_bitcast_fusion.5
  404.4 0.8 dynamic-slice_bitcast_fusion.4
  408.9 0.7 dynamic-slice_bitcast_fusion.5
  409.6 0.8 dynamic-slice_bitcast_fusion.4
  414.1 0.7 dynamic-slice_bitcast_fusion.5
  414.8 0.8 dynamic-slice_bitcast_fusion.4
  419.2 0.7 dynamic-slice_bitcast_fusion.5
  420.0 0.8 dynamic-slice_bitcast_fusion.4
  424.4 0.7 dynamic-slice_bitcast_fusion.5
  425.2 0.8 dynamic-slice_bitcast_fusion.4
  429.6 0.7 dynamic-slice_bitcast_fusion.5
  430.3 0.8 dynamic-slice_bitcast_fusion.4
  435.5 0.8 dynamic-slice_bitcast_fusion.4
  440.7 0.8 dynamic-slice_bitcast_fusion.4
  445.2 0.7 dynamic-slice_bitcast_fusion.5
  445.9 0.8 dynamic-slice_bitcast_fusion.4
  450.4 0.7 dynamic-slice_bitcast_fusion.5
  451.1 0.8 dynamic-slice_bitcast_fusion.4
  454.3 1.9 copy.56
  456.2 27.8 %all_to_all.60 = bf16[16,256,128]{2,0,1:T(8,128)(2,1)S(1)} all-to-all(bf16[16,256,128]{2,0,1:T(8,128)(2,1)S(1)} %copy.56), channel_id=1, replica_groups=mesh['grp'=2,'seq'=4,'head'=4] {'seq'}, dimensions={1} | all-to-all | bytes 2097152 | tf_op jit(solution)/shard_map/all_to_all | solution.py:112
  484.3 1.5 fusion.25
  486.5 1.6 reshape_reshape.7
  488.0 1.9 copy.58
  489.9 1.5 reshape_reshape.6
  491.4 5.9 %fusion.27 = f32[256,4096]{1,0:T(8,128)S(1)} fusion(bf16[256,1024]{1,0:T(8,128)(2,1)} %reshape_reshape.6, bf16[4096,1024]{0,1:T(8,128)(2,1)} %all-gather.3.cloned.1.call-done), kind=kOutput, calls=%fused_computation.52 | convolution fusion | flops 2147483648 | bytes 13107200 | tf_op jit(solution)/shard_map/dot_general | solution.py:52
  497.4 7.8 %convolution_add_fusion = f32[256,4096]{1,0:T(8,128)} fusion(f32[256,4096]{1,0:T(8,128)S(1)} %fusion.27, bf16[256,1024]{1,0:T(8,128)(2,1)S(1)} %copy-done.1, bf16[4096,1024]{0,1:T(8,128)(2,1)} %all-gather.5.cloned.1.call-done), kind=kOutput, calls=%fused_computation.31 | convolution fusion | flops 2148532224 | bytes 17301504 | tf_op jit(solution)/shard_map/dot_general | solution.py:53
  505.4 10.8 %all_to_all.61 = bf16[16,64,128]{2,0,1:T(8,128)(2,1)S(1)} all-to-all(bf16[16,64,128]{2,0,1:T(8,128)(2,1)S(1)} %copy.55), channel_id=1, replica_groups=mesh['grp'=2,'seq'=4,'head'=4] {'seq'}, dimensions={1} | all-to-all | bytes 524288 | tf_op jit(solution)/shard_map/all_to_all | solution.py:111
  516.4 0.9 reshape.86
  517.2 0.9 reshape.85
  518.1 30.9 %reduce-scatter.2.cloned.1.call-done = f32[256,1024]{1,0:T(8,128)} async-done(((f32[256,4096]{1,0:T(8,128)}), f32[256,1024]{1,0:T(8,128)}) %reduce-scatter.2.cloned.1.call-update) | async-done | bytes 1048592 | tf_op jit(solution)/shard_map/reduce_scatter | solution.py:119
  549.0 2.1 convert_element_type.80
  (215 shorter events, 62.0 us)
Async XLA Ops:
  7.2 166.3 %copy-start = (bf16[4,64,4096]{2,1,0:T(8,128)(2,1)S(1)}, bf16[4,64,4096]{2,1,0:T(8,128)(2,1)}, u32[]{:S(2)}) copy-start(bf16[4,64,4096]{2,1,0:T(8,128)(2,1)} %param.9) | copy-start | bytes 6291460
  7.2 166.3 %all-gather.3.cloned.1.call-start = ((), (), s32[]{:S(2)}) async-start(), calls=%async_computation.5 | async-start | bytes 10485760 | tf_op jit(solution)/shard_map/all_gather | solution.py:68
  15.4 307.4 %all-gather.5.cloned.1.call-start = ((), (), s32[]{:S(2)}) async-start(), calls=%async_computation.6 | async-start | bytes 10485760 | tf_op jit(solution)/shard_map/all_gather | solution.py:69
  22.8 0.9 copy-start.3
  22.8 1.1 copy-start.4
  25.0 315.6 %all-to-all-start = ((bf16[64,16,128]{2,1,0:T(8,128)(2,1)}), bf16[64,16,128]{2,1,0:T(8,128)(2,1)S(1)}, u32[]{:S(2)}, u32[]{:S(2)}) async-start(bf16[64,16,128]{2,1,0:T(8,128)(2,1)} %bitcast.6), calls=%async_computation | async-start | bytes 524288 | tf_op jit(solution)/shard_map/all_to_all | solution.py:90
  337.7 6.4 %copy-start.5 = (s32[4]{0:T(128)S(1)}, s32[4]{0:T(128)}, u32[]{:S(2)}) copy-start(s32[4]{0:T(128)} %param.13) | copy-start | bytes 52
  340.6 29.7 %all-to-all-start.1 = ((bf16[64,64,128]{2,1,0:T(8,128)(2,1)}), bf16[64,64,128]{2,1,0:T(8,128)(2,1)S(1)}, u32[]{:S(2)}, u32[]{:S(2)}) async-start(bf16[64,64,128]{2,1,0:T(8,128)(2,1)} %bitcast.18), calls=%async_computation.1 | async-start | bytes 2097152 | tf_op jit(solution)/shard_map/all_to_all | solution.py:92
  344.1 204.9 %reduce-scatter.2.cloned.1.call-start = ((), (), s32[]{:S(2)}) async-start(), calls=%async_computation.7 | async-start | bytes 5242880 | tf_op jit(solution)/shard_map/reduce_scatter | solution.py:119
  345.0 26.3 %copy-start.2 = (bf16[16,64,128]{2,1,0:T(8,128)(2,1)S(1)}, bf16[16,64,128]{2,1,0:T(8,128)(2,1)}, u32[]{:S(2)}) copy-start(bf16[16,64,128]{2,1,0:T(8,128)(2,1)} %custom-call) | copy-start | bytes 786436
  491.4 6.0 %copy-start.1 = (bf16[256,1024]{1,0:T(8,128)(2,1)S(1)}, bf16[256,1024]{1,0:T(8,128)(2,1)}, u32[]{:S(2)}) copy-start(bf16[256,1024]{1,0:T(8,128)(2,1)} %reshape_reshape.7) | copy-start | bytes 1572868
Sparse Core Ops, SparseCore 0:
  15.5 157.8 all-gather.2
  175.1 147.7 all-gather.4
  505.4 43.5 reduce-scatter.1
where the time goes:
time: 560 us; the launch traced here: 558 us
  waiting for transfers between devices  342 us (61%)
  local copies, waits for them, and re-layouts  66.4 us (12%)
  matrix products  48.8 us (9%)
  blocking collectives  38.6 us (7%)
  other arithmetic  37.3 us (7%)
  between operations  13.9 us (2%)
  starting transfers between devices  9.98 us (2%)
    all_gather x1, waiting for transfers between devices, body(): lax.all_gather(value_masked, 'seq', axis=0, tiled=True)  144 us
    all_gather x1, waiting for transfers between devices, body(): lax.all_gather(key_masked, 'seq', axis=0, tiled=True)  142 us
    reduce_scatter x1, waiting for transfers between devices, body(): lax.psum_scatter(grad_terms, 'head', scatter_dimension=1, tiled=True)  30.9 us
    all_to_all x1, blocking collectives, body(): lax.all_to_all(back, 'seq', split_axis=1, concat_axis=0, tiled=True)  27.8 us
    all_to_all x1, waiting for transfers between devices, body(): lax.all_to_all(kv_pairs, 'seq', split_axis=0, concat_axis=1, tiled=True)  25.3 us
    squeeze x32, local copies, waits for them, and re-layouts, body(): front, back = lax.map(owner_pair, (kv_owned, query_owned, pair_length))  25.1 us
    dynamic_update_slice x32, other arithmetic, body(): front, back = lax.map(owner_pair, (kv_owned, query_owned, pair_length))  11.7 us
  transfers between devices with their start and end apart: 5, of which 4 were waited for; matrix products, arithmetic and copies ran while one was open for 6% of the time, Pallas kernels for 0%

commit v1 on v0

--- a/solution.py
+++ b/solution.py
@@ -8,6 +8,24 @@
 DOCS = 4
 SCALE = 0.125
 FLOOR_SCORE = -1e30
+
+
+def gather_around(value, axis, dim):
+    ways, here, lap = (lax.axis_size(axis), lax.axis_index(axis), value.shape[dim])
+    shape = [n * ways if d == dim else n for d, n in enumerate(value.shape)]
+    full = lax.dynamic_update_slice_in_dim(
+        jnp.zeros(shape, value.dtype), value, here * lap, axis=dim
+    )
+    going_up = going_down = value
+    for far in range(1, ways // 2 + 1):
+        going_up = lax.ppermute(going_up, axis, [(d, (d + 1) % ways) for d in range(ways)])
+        full = lax.dynamic_update_slice_in_dim(full, going_up, (here - far) % ways * lap, axis=dim)
+        if 2 * far < ways:
+            going_down = lax.ppermute(going_down, axis, [(d, (d - 1) % ways) for d in range(ways)])
+            full = lax.dynamic_update_slice_in_dim(
+                full, going_down, (here + far) % ways * lap, axis=dim
+            )
+    return full
 
 
 def expand(tile_grid, tile_edge):
@@ -65,7 +83,7 @@
     key_masked = key_weight * expand(tile_mask[0], TILE).astype(jnp.bfloat16)
     value_masked = value_weight * expand(tile_mask[1], TILE).astype(jnp.bfloat16)
     full_key, full_value = (
-        lax.all_gather(key_masked, "seq", axis=0, tiled=True),
+        gather_around(key_masked, "seq", 0),
         lax.all_gather(value_masked, "seq", axis=0, tiled=True),
     )
     key_sum, value_sum = project(encoder, full_key, full_value)

time: 560 us -> 524 us (0.936)
  waiting for transfers between devices: 342 us -> 223 us
  starting transfers between devices: 9.98 us -> 102 us
  local copies, waits for them, and re-layouts: 66.4 us -> 58.7 us
    ppermute x0 -> x3, waiting for transfers between devices: none -> 170 us  [the longest x2 170 us: gather_around(): lax.ppermute(going_up, axis, [(d, (d + 1) % ways) for d in range(ways)])]
    all_gather x1, waiting for transfers between devices: 144 us -> 0.02 us  [body(): lax.all_gather(value_masked, 'seq', axis=0, tiled=True)]
    all_gather x1 -> x0, waiting for transfers between devices: 142 us -> none  [body(): lax.all_gather(key_masked, 'seq', axis=0, tiled=True)]
    ppermute x0 -> x3, starting transfers between devices: none -> 88.7 us  [the longest x2 86.5 us: gather_around(): lax.ppermute(going_up, axis, [(d, (d + 1) % ways) for d in range(ways)])]
    squeeze x32, local copies, waits for them, and re-layouts: 25.1 us -> 11.7 us  [body(): front, back = lax.map(owner_pair, (kv_owned, query_owned, pair_length))]
    dynamic_update_slice x0 -> x3, local copies, waits for them, and re-layouts: none -> 9.34 us  [the longest x2 6.25 us: gather_around(): lax.dynamic_update_slice_in_dim(full, going_up, (here - far) % ways * lap...]
  transfers between devices with their start and end apart: 5 -> 7, of which waited for: 4 -> 4; matrix products, arithmetic and copies ran while one was open for 6% -> 9% of each run, Pallas kernels for 0% -> 0%
where the time goes in v1:
time: 524 us; the launch traced here: 522 us
  waiting for transfers between devices  223 us (43%)
  starting transfers between devices  102 us (19%)
  local copies, waits for them, and re-layouts  58.7 us (11%)
  matrix products  48.4 us (9%)
  blocking collectives  38.6 us (7%)
  other arithmetic  35.6 us (7%)
  between operations  14.3 us (3%)
    ppermute x2, waiting for transfers between devices, gather_around(): lax.ppermute(going_up, axis, [(d, (d + 1) % ways) for d in range(ways)])  170 us
    ppermute x2, starting transfers between devices, gather_around(): lax.ppermute(going_up, axis, [(d, (d + 1) % ways) for d in range(ways)])  86.5 us
    reduce_scatter x1, waiting for transfers between devices, body(): lax.psum_scatter(grad_terms, 'head', scatter_dimension=1, tiled=True)  29.8 us
    all_to_all x1, blocking collectives, body(): lax.all_to_all(back, 'seq', split_axis=1, concat_axis=0, tiled=True)  27.7 us
    all_to_all x1, waiting for transfers between devices, body(): lax.all_to_all(kv_pairs, 'seq', split_axis=0, concat_axis=1, tiled=True)  23.6 us
    squeeze x32, local copies, waits for them, and re-layouts, body(): front, back = lax.map(owner_pair, (kv_owned, query_owned, pair_length))  11.7 us
    dynamic_update_slice x32, other arithmetic, body(): front, back = lax.map(owner_pair, (kv_owned, query_owned, pair_length))  11.4 us
    all_to_all x1, blocking collectives, body(): lax.all_to_all(front, 'seq', split_axis=1, concat_axis=0, tiled=True)  10.9 us
  transfers between devices with their start and end apart: 7, of which 4 were waited for; matrix products, arithmetic and copies ran while one was open for 9% of the time, Pallas kernels for 0%

profile of v1, /device:TPU:0, one launch (start us, length us, event | category | flops | bytes accessed | tf_op | source)
XLA Modules:
  0.0 522.2 jit_solution(1714573954453987035)
XLA Ops:
  7.2 0.9 convert.4
  8.4 4.0 copy.51
  12.4 3.1 bitcast_multiply_fusion
  15.8 3.9 copy.49
  19.8 4.3 broadcast_in_dim.70
  24.0 2.9 constant_dynamic-update-slice_fusion.3
  26.9 3.0 collective-permute-start
  29.9 2.2 collective-permute-start.1
  32.1 91.5 %collective-permute-done = bf16[1024,1024]{0,1:T(8,128)(2,1)} collective-permute-done((bf16[1024,1024]{0,1:T(8,128)(2,1)}, bf16[1024,1024]{0,1:T(8,128)(2,1)}, u32[]{:S(2)}, u32[]{:S(2)}) %collective-permute-start) | collective-permute-done | bytes 2097184 | tf_op jit(solution)/shard_map/ppermute | solution.py:21
  123.6 83.6 %collective-permute-start.2 = (bf16[1024,1024]{0,1:T(8,128)(2,1)}, bf16[1024,1024]{0,1:T(8,128)(2,1)}, u32[]{:S(2)}, u32[]{:S(2)}) collective-permute-start(bf16[1024,1024]{0,1:T(8,128)(2,1)} %collective-permute-done), channel_id=1, source_target_pairs={{0,4},{4,8},{8,12},{12,0},{1,5},{5,9},{9,13},{13,1},{2,6},{6,10},{... | collective-permute-start | bytes 6291464 | tf_op jit(solution)/shard_map/ppermute | solution.py:21
  207.7 0.8 copy.46
  208.5 9.9 %all-to-all-start = ((bf16[64,16,128]{2,1,0:T(8,128)(2,1)}), bf16[64,16,128]{2,1,0:T(8,128)(2,1)S(1)}, u32[]{:S(2)}, u32[]{:S(2)}) async-start(bf16[64,16,128]{2,1,0:T(8,128)(2,1)} %bitcast.6), calls=%async_computation | async-start | bytes 524288 | tf_op jit(solution)/shard_map/all_to_all | solution.py:108
  218.4 3.2 constant_dynamic-update-slice_fusion.2
  221.6 3.1 constant_dynamic-update-slice_fusion.1
  224.7 78.2 %collective-permute-done.2 = bf16[1024,1024]{0,1:T(8,128)(2,1)} collective-permute-done((bf16[1024,1024]{0,1:T(8,128)(2,1)}, bf16[1024,1024]{0,1:T(8,128)(2,1)}, u32[]{:S(2)}, u32[]{:S(2)}) %collective-permute-start.2) | collective-permute-done | bytes 2097184 | tf_op jit(solution)/shard_map/ppermute | solution.py:21
  302.9 3.1 constant_dynamic-update-slice_fusion
  306.0 5.8 %fusion.21 = bf16[256,1024]{0,1:T(8,128)(2,1)S(1)} fusion(bf16[4096,1024]{0,1:T(8,128)(2,1)} %constant_dynamic-update-slice_fusion, bf16[256,4096]{1,0:T(8,128)(2,1)S(1)} %bitcast.87), kind=kOutput, calls=%fused_computation.36 | convolution fusion | flops 2147745792 | bytes 11010048 | tf_op jit(solution)/shard_map/dot_general | solution.py:62
  311.8 1.4 convert_element_type.73
  313.2 1.7 copy.52
  314.9 6.5 %fusion.22 = bf16[256,1024]{0,1:T(8,128)(2,1)} fusion(bf16[4096,1024]{0,1:T(8,128)(2,1)} %all-gather.2.cloned.1.call-done, bf16[256,4096]{1,0:T(8,128)(2,1)S(1)} %bitcast.88), kind=kOutput, calls=%fused_computation.37 | convolution fusion | flops 2147745792 | bytes 11010048 | tf_op jit(solution)/shard_map/dot_general | solution.py:63
  321.5 2.0 convert_element_type.79
  323.5 0.8 copy.53
  324.3 1.6 pad_maximum_fusion
  325.9 3.5 all-to-all-start.1
  329.8 0.7 copy.47
  330.5 23.6 %all-to-all-done.1 = bf16[64,64,128]{2,1,0:T(8,128)(2,1)S(1)} async-done(((bf16[64,64,128]{2,1,0:T(8,128)(2,1)}), bf16[64,64,128]{2,1,0:T(8,128)(2,1)S(1)}, u32[]{:S(2)}, u32[]{:S(2)}) %all-to-all-start.1) | async-done | bytes 1048608 | tf_op jit(solution)/shard_map/all_to_all | solution.py:110
  354.2 69.4 %while.12 = (s32[]{:T(128)}, bf16[16,64,128]{2,1,0:T(8,128)(2,1)}, bf16[16,256,128]{1,2,0:T(8,128)(2,1)S(1)}, s32[16]{0:T(128)S(1)}, bf16[16,64,128]{2,1,0:T(8,1...) while((s32[]{:T(128)}, bf16[16,64,128]{2,1,0:T(8,128)(2,1)}, bf16[16,256,128]{1,2,0:T(8,128)(2,1)S(1)}, ...), condition=%wide.region_5.6_spmd, body=%wide.region_1.5_spmd.sunk | while | flops 13144130 | bytes 1176425 | solution.py:127
  354.2 0.7 dynamic-slice_bitcast_fusion.5
  357.9 0.7 fusion.64
  358.6 0.7 dynamic-slice_bitcast_fusion.5
  362.2 0.7 fusion.64
  362.9 0.7 dynamic-slice_bitcast_fusion.5
  366.5 0.7 fusion.64
  367.2 0.7 dynamic-slice_bitcast_fusion.5
  370.9 0.7 fusion.64
  371.6 0.7 dynamic-slice_bitcast_fusion.5
  375.2 0.7 fusion.64
  375.9 0.7 dynamic-slice_bitcast_fusion.5
  379.5 0.7 fusion.64
  380.2 0.7 dynamic-slice_bitcast_fusion.5
  383.9 0.7 fusion.64
  384.6 0.7 dynamic-slice_bitcast_fusion.5
  388.2 0.7 fusion.64
  388.9 0.7 dynamic-slice_bitcast_fusion.5
  393.2 0.7 dynamic-slice_bitcast_fusion.5
  396.9 0.7 fusion.64
  397.6 0.7 dynamic-slice_bitcast_fusion.5
  401.9 0.7 dynamic-slice_bitcast_fusion.5
  406.2 0.7 dynamic-slice_bitcast_fusion.5
  410.6 0.7 dynamic-slice_bitcast_fusion.5
  414.9 0.7 dynamic-slice_bitcast_fusion.5
  419.3 0.7 dynamic-slice_bitcast_fusion.5
  423.6 1.1 copy.56
  424.7 27.7 %all_to_all.60 = bf16[16,256,128]{2,0,1:T(8,128)(2,1)S(1)} all-to-all(bf16[16,256,128]{2,0,1:T(8,128)(2,1)S(1)} %copy.56), channel_id=1, replica_groups=mesh['grp'=2,'seq'=4,'head'=4] {'seq'}, dimensions={1} | all-to-all | bytes 2097152 | tf_op jit(solution)/shard_map/all_to_all | solution.py:130
  453.8 0.7 reshape_reshape.7
  455.3 0.7 reshape_reshape.6
  456.0 5.7 %fusion.27 = f32[256,4096]{1,0:T(8,128)S(1)} fusion(bf16[256,1024]{1,0:T(8,128)(2,1)S(1)} %reshape_reshape.7, bf16[4096,1024]{0,1:T(8,128)(2,1)} %all-gather.2.cloned.1.call-done), kind=kOutput, calls=%fused_computation.56 | convolution fusion | flops 2147483648 | bytes 13107200 | tf_op jit(solution)/shard_map/dot_general | solution.py:71
  461.7 7.8 %convolution_add_fusion = f32[256,4096]{1,0:T(8,128)} fusion(f32[256,4096]{1,0:T(8,128)S(1)} %fusion.27, bf16[256,1024]{1,0:T(8,128)(2,1)S(1)} %reshape_reshape.6, bf16[4096,1024]{0,1:T(8,128)(2,1)} %constant_dynamic-update-slice_fusion), kind=kOutput, calls=%fused_computation.31 | convolution fusion | flops 2148532224 | bytes 17301504 | tf_op jit(solution)/shard_map/dot_general | solution.py:70
  469.5 0.9 copy-done.3
  470.6 10.9 %all_to_all.61 = bf16[16,64,128]{2,0,1:T(8,128)(2,1)S(1)} all-to-all(bf16[16,64,128]{2,0,1:T(8,128)(2,1)S(1)} %copy.55), channel_id=1, replica_groups=mesh['grp'=2,'seq'=4,'head'=4] {'seq'}, dimensions={1} | all-to-all | bytes 524288 | tf_op jit(solution)/shard_map/all_to_all | solution.py:129
  481.7 0.9 reshape.85
  482.5 0.9 reshape.86
  483.4 29.8 %reduce-scatter.2.cloned.1.call-done = f32[256,1024]{1,0:T(8,128)} async-done(((f32[256,4096]{1,0:T(8,128)}), f32[256,1024]{1,0:T(8,128)}) %reduce-scatter.2.cloned.1.call-update) | async-done | bytes 1048592 | tf_op jit(solution)/shard_map/reduce_scatter | solution.py:137
  513.2 2.1 convert_element_type.80
  (224 shorter events, 54.8 us)
Async XLA Ops:
  7.2 298.8 %copy-start = (bf16[4,64,4096]{2,1,0:T(8,128)(2,1)S(1)}, bf16[4,64,4096]{2,1,0:T(8,128)(2,1)}, u32[]{:S(2)}) copy-start(bf16[4,64,4096]{2,1,0:T(8,128)(2,1)} %param.9) | copy-start | bytes 6291460
  7.2 307.7 %all-gather.2.cloned.1.call-start = ((), (), s32[]{:S(2)}) async-start(), calls=%async_computation.5 | async-start | bytes 10485760 | tf_op jit(solution)/shard_map/all_gather | solution.py:87
  19.7 4.3 copy-start.2
  24.0 183.1 %copy-start.4 = (bf16[4,16,1024]{2,1,0:T(8,128)(2,1)S(1)}, bf16[4,16,1024]{2,1,0:T(8,128)(2,1)}, u32[]{:S(2)}) copy-start(bf16[4,16,1024]{2,1,0:T(8,128)(2,1)} %param.14) | copy-start | bytes 393220
  24.0 183.3 %copy-start.5 = (bf16[4,16,1024]{2,1,0:T(8,128)(2,1)S(1)}, bf16[4,16,1024]{2,1,0:T(8,128)(2,1)}, u32[]{:S(2)}) copy-start(bf16[4,16,1024]{2,1,0:T(8,128)(2,1)} %param.15) | copy-start | bytes 393220
  26.9 96.6 %collective-permute-start = (bf16[1024,1024]{0,1:T(8,128)(2,1)}, bf16[1024,1024]{0,1:T(8,128)(2,1)}, u32[]{:S(2)}, u32[]{:S(2)}) collective-permute-start(bf16[1024,1024]{0,1:T(8,128)(2,1)} %get-tuple-element.61), channel_id=1, source_target_pairs={{0,4},{4,8},{8,12},{12,0},{1,5},{5,9},{9,13},{13,1},{2,6},{6,10},{... | collective-permute-start | bytes 6291464 | tf_op jit(solution)/shard_map/ppermute | solution.py:21
  29.9 191.7 %collective-permute-start.1 = (bf16[1024,1024]{0,1:T(8,128)(2,1)}, bf16[1024,1024]{0,1:T(8,128)(2,1)}, u32[]{:S(2)}, u32[]{:S(2)}) collective-permute-start(bf16[1024,1024]{0,1:T(8,128)(2,1)} %get-tuple-element.61), channel_id=1, source_target_pairs={{0,12},{4,0},{8,4},{12,8},{1,13},{5,1},{9,5},{13,9},{2,14},{6,2},{... | collective-permute-start | bytes 6291464 | tf_op jit(solution)/shard_map/ppermute | solution.py:24
  123.6 179.3 %collective-permute-start.2 = (bf16[1024,1024]{0,1:T(8,128)(2,1)}, bf16[1024,1024]{0,1:T(8,128)(2,1)}, u32[]{:S(2)}, u32[]{:S(2)}) collective-permute-start(bf16[1024,1024]{0,1:T(8,128)(2,1)} %collective-permute-done), channel_id=1, source_target_pairs={{0,4},{4,8},{8,12},{12,0},{1,5},{5,9},{9,13},{13,1},{2,6},{6,10},{... | collective-permute-start | bytes 6291464 | tf_op jit(solution)/shard_map/ppermute | solution.py:21
  208.5 117.4 %all-to-all-start = ((bf16[64,16,128]{2,1,0:T(8,128)(2,1)}), bf16[64,16,128]{2,1,0:T(8,128)(2,1)S(1)}, u32[]{:S(2)}, u32[]{:S(2)}) async-start(bf16[64,16,128]{2,1,0:T(8,128)(2,1)} %bitcast.6), calls=%async_computation | async-start | bytes 524288 | tf_op jit(solution)/shard_map/all_to_all | solution.py:108
  321.5 8.2 %copy-start.6 = (s32[4]{0:T(128)S(1)}, s32[4]{0:T(128)}, u32[]{:S(2)}) copy-start(s32[4]{0:T(128)} %param.13) | copy-start | bytes 52
  325.9 28.2 %all-to-all-start.1 = ((bf16[64,64,128]{2,1,0:T(8,128)(2,1)}), bf16[64,64,128]{2,1,0:T(8,128)(2,1)S(1)}, u32[]{:S(2)}, u32[]{:S(2)}) async-start(bf16[64,64,128]{2,1,0:T(8,128)(2,1)} %bitcast.18), calls=%async_computation.1 | async-start | bytes 2097152 | tf_op jit(solution)/shard_map/all_to_all | solution.py:110
  329.4 183.8 %reduce-scatter.2.cloned.1.call-start = ((), (), s32[]{:S(2)}) async-start(), calls=%async_computation.6 | async-start | bytes 5242880 | tf_op jit(solution)/shard_map/reduce_scatter | solution.py:137
  469.5 0.9 copy-start.3
  469.5 45.8 %copy-start.1 = (bf16[4,64,4096]{2,1,0:T(8,128)(2,1)S(1)}, bf16[4,64,4096]{2,1,0:T(8,128)(2,1)}, u32[]{:S(2)}) copy-start(bf16[4,64,4096]{2,1,0:T(8,128)(2,1)} %param.9) | copy-start | bytes 6291460
Sparse Core Ops, SparseCore 0:
  15.6 292.2 all-gather.1
  469.7 43.5 reduce-scatter.1
